TPU v7x, 32 devices: a whole 2x2x4 slice. The times are simulated.
32 devices in a mesh: groups: 2 (over x), req: 16 (over z, y, core).
Axes of the slice: x: 2, y: 2, z: 4, core: 2. Of those that a mesh axis runs over, the one named last changes fastest.
Arguments:
- queries: bfloat16 [64, 128, 192], P('groups', 'req'), parts along dimension 0, may hold values from -48 to 48
- absorb_key: bfloat16 [128, 128, 512], P('req'), may hold values from -0.5 to 0.5
- absorb_value: bfloat16 [128, 512, 128], P('req'), may hold values from -0.75 to 0.75
- out_weight: bfloat16 [16384, 5120], P('req'), may hold values from -0.046875 to 0.046875
- latent_cache: bfloat16 [64, 4096, 576], P(('groups', 'req')), parts along dimension 0, may hold values from -12 to 12
- lengths: int32 [64], P(('groups', 'req')), parts along dimension 0, may hold values from 2 to 4096, as said below
- slot_request: int32 [64], P('groups'), parts along dimension 0, may hold values from 0 to 31, each once
Outputs:
- attended: bfloat16 [64, 5120], P(('groups', 'req')), parts along dimension 0
There are 2 independent parts, one for each index of `groups`. A program takes and returns all parts, laid end to end along the dimension named above; an argument that names none is the same for every part. Nothing has to cross between parts.
Inputs may be any that keep to these rules, and one draw needn't show every extreme that they name: Slot j's valid positions are its first lengths[j] ones; some slot of each group holds exactly 4096. `slot_request`: each request stands in exactly one slot.
All inputs are finite; a program needn't handle non-finite values.
Results may differ from a plain program's by a relative error of at most 0.0079.
Values may be sent and summed in bfloat16 or wider, within the bound.
A program may use at most 64 MiB of HBM per device.

v0:
```python
import functools
import math

import jax
import jax.numpy as jnp
from jax import lax
from jax.experimental import pallas as pl
from jax.experimental.pallas import tpu as pltpu
from jax.sharding import PartitionSpec as P

MESH = pl.DeviceIdType.MESH
LANES = 128
CORES = 2
SCORE_TILE = 1024
COLUMNS = 2


def pieces_of(slots, heads):
    whole = [(s, 0, heads) for s in range(slots - 1)]
    return whole + [(slots - 1, 0, heads)]


def far_first(mine, count, width):
    block, place, blocks = lax.div(mine, width), lax.rem(mine, width), count // width
    low = (block < blocks // 2).astype(jnp.int32)
    for i in range(blocks - 1):
        down = blocks - 1 - i - (blocks - 1 - i <= block).astype(jnp.int32)
        up = i + (i >= block).astype(jnp.int32)
        chosen = low * down + (1 - low) * up
        for j in range(width):
            yield chosen * width + lax.rem(place + j, width)
    for j in range(1, width):
        yield block * width + lax.rem(place + j, width)


def kernel(n, pieces, request_hbm, length_hbm, query_hbm, key_hbm, value_hbm, weight_hbm, cache_hbm, out_ref, *scratch):
    parts = len(pieces)
    scratch = list(scratch)
    take = lambda count: [scratch.pop(0) for _ in range(count)]
    request_ref, length_ref, query_ref, key, value, weight, cache = take(7)
    query_rows, rotary_rows, absorbed_rows, slot_rows, scores, latent_rows, returned_rows = take(7)
    absorbed_out, absorbed_in, latent_out, latent_in = take(parts), take(parts), take(parts), take(parts)
    carried, partial, partner_rows, partial_out, partial_in = take(5)
    small_sem, load_sem, send_a, recv_a, send_b, recv_b, send_p, recv_p, send_c, recv_c = take(10)

    requests, heads, width = query_ref.shape
    nope, latent = key_hbm.shape[1:]
    vdim = value_hbm.shape[2]
    slots, _, context = cache_hbm.shape
    rope = width - nope
    lanes = latent // LANES
    chips = n // CORES
    me = lax.axis_index("req")

    barrier = pltpu.get_barrier_semaphore()

    for k in range(1, n):
        pl.semaphore_signal(
            barrier, inc=1, device_id={"req": lax.rem(me + k, n)}, device_id_type=MESH
        )

    small = [
        pltpu.make_async_copy(source, into, small_sem.at[i])
        for i, (source, into) in enumerate(
            [(request_hbm, request_ref), (query_hbm, query_ref), (length_hbm, length_ref)]
        )
    ]
    for load in small:
        load.start()
    load_key = pltpu.make_async_copy(key_hbm, key, load_sem.at[0])
    load_value = pltpu.make_async_copy(value_hbm, value, load_sem.at[1])
    load_weight = pltpu.make_async_copy(weight_hbm, weight, load_sem.at[2])
    load_cache = [
        pltpu.make_async_copy(cache_hbm.at[s], cache.at[s], load_sem.at[3 + s])
        for s in range(slots)
    ]
    load_key.start()
    load_cache[0].start()

    for load in small:
        load.wait()
    for j in range(requests):
        row = query_ref[request_ref[j]].astype(jnp.float32)
        query_rows[j * heads : (j + 1) * heads, :] = row[:, :nope]
        rotary_rows[j * heads : (j + 1) * heads, :] = row[:, nope:]
    load_key.wait()
    for s in range(1, slots):
        load_cache[s].start()
    load_value.start()
    load_weight.start()
    for h in range(heads):
        picked = query_rows[pl.ds(h, requests, stride=heads), :].astype(jnp.bfloat16)
        lifted = jnp.dot(picked, key[h], preferred_element_type=jnp.float32)
        for l in range(lanes):
            absorbed_rows[l, pl.ds(h, requests, stride=heads), :] = lifted[
                :, l * LANES : (l + 1) * LANES
            ]

    def exchange(out, into, send_sem, recv_sem, stride=1):
        mine, count = lax.div(me, stride), n // stride

        def copy(to, source, block):
            return pltpu.make_async_remote_copy(
                src_ref=out.at[block + (to,)],
                dst_ref=into.at[block + (source,)],
                send_sem=send_sem,
                recv_sem=recv_sem,
                device_id={"req": to * stride + lax.rem(me, stride)},
                device_id_type=MESH,
            )

        def start(*block):
            for to in far_first(mine, count, 2 * CORES // stride):
                copy(to, mine, block).start()

        def others(ref):
            block = ref.at[(slice(None),) * (len(ref.shape) - 3) + (pl.ds(0, count - 1),)]
            return pltpu.make_async_copy(block, block, recv_sem if ref is into else send_sem)

        def arrive():
            others(into).wait()

        def leave():
            others(out).wait()

        return start, arrive, leave

    queries_of = [
        exchange(absorbed_out[p], absorbed_in[p], send_a.at[p], recv_a.at[p]) for p in range(parts)
    ]
    latents_of = [
        exchange(latent_out[p], latent_in[p], send_b.at[p], recv_b.at[p]) for p in range(parts)
    ]
    partials_of = [
        exchange(partial_out.at[s], partial_in.at[s], send_c.at[s], recv_c.at[s], CORES)
        for s in range(slots)
    ]

    for p, (s, first, end) in enumerate(pieces):
        for d in range(n):
            row = (d * slots + s) * heads
            for l in range(lanes):
                absorbed_out[p][d, :, l * LANES : (l + 1) * LANES] = absorbed_rows[
                    l, row + first : row + end, :
                ].astype(jnp.bfloat16)
            if p == 0:
                rotary = [
                    rotary_rows[(d * slots + i) * heads : (d * slots + i + 1) * heads, :]
                    for i in range(slots)
                ]
                absorbed_out[p][d, :, latent:] = jnp.concatenate(rotary, axis=1).astype(jnp.bfloat16)
        if p == 0:
            pl.semaphore_wait(barrier, n - 1)
        queries_of[p][0]()
        absorbed_in[p][me] = absorbed_out[p][me]

    scale = math.log2(math.e) / math.sqrt(width)
    for p, (s, first, end) in enumerate(pieces):
        count = end - first
        rows = n * count
        queries_of[p][1]()
        for i in range(n):
            slot_rows[i * count : (i + 1) * count, :latent] = absorbed_in[p][i, :, :latent].astype(
                jnp.float32
            )
            rotary = absorbed_in[0][i, :, latent:].astype(jnp.float32)
            slot_rows[i * count : (i + 1) * count, latent:] = rotary[
                first:end, s * rope : (s + 1) * rope
            ]
        query = slot_rows[:rows, :].astype(jnp.bfloat16)
        if first == 0:
            load_cache[s].wait()
        length = length_ref[s]
        highest = None
        for t in range(0, context, SCORE_TILE):
            score = jnp.dot(
                query, cache[s, :, t : t + SCORE_TILE], preferred_element_type=jnp.float32
            )
            position = t + lax.broadcasted_iota(jnp.int32, (1, SCORE_TILE), 1)
            score = jnp.where(position < length, score, -jnp.inf)
            scores[:rows, t : t + SCORE_TILE] = score
            top = jnp.max(score, axis=1, keepdims=True)
            highest = top if highest is None else jnp.maximum(highest, top)
        total, mixed = None, None
        for t in range(0, context, SCORE_TILE):
            prob = jnp.exp2((scores[:rows, t : t + SCORE_TILE] - highest) * scale)
            part = jnp.sum(prob, axis=1, keepdims=True)
            product = lax.dot_general(
                prob.astype(jnp.bfloat16),
                cache[s, :latent, t : t + SCORE_TILE],
                (((1,), (1,)), ((), ())),
                preferred_element_type=jnp.float32,
            )
            total = part if total is None else total + part
            mixed = product if mixed is None else mixed + product
        latent_rows[:rows, :] = mixed / total
        for i in range(n):
            latent_out[p][i] = latent_rows[i * count : (i + 1) * count, :].astype(jnp.bfloat16)
        latents_of[p][0]()
        latent_in[p][me] = latent_out[p][me]

    core, chip = lax.rem(me, CORES), lax.div(me, CORES)
    model = out_ref.shape[1]
    span = model // COLUMNS
    half = span // 2

    def pair(s, k):
        return pltpu.make_async_remote_copy(
            src_ref=partial.at[s, k, CORES - 1 - core],
            dst_ref=partner_rows.at[s, k],
            send_sem=send_p.at[s, k],
            recv_sem=recv_p.at[s, k],
            device_id={"req": me + CORES - 1 - 2 * core},
            device_id_type=MESH,
        )

    waiting = []

    def finish(s, k):
        pair(s, k).wait_recv()
        chip_rows = partial[s, k, core] + partner_rows[s, k]
        for e in range(chips):
            partial_out[s, k, e] = jnp.concatenate(
                [chip_rows[e : e + 1, :half], chip_rows[e : e + 1, half:]], axis=0
            ).astype(jnp.bfloat16)
        partials_of[s][0](k)
        partial_in[s, k, chip] = partial_out[s, k, chip]

    load_value.wait()
    load_weight.wait()
    for p, (s, first, end) in enumerate(pieces):
        count = end - first
        latents_of[p][1]()
        for d in range(n):
            row = ((d % CORES) * chips + d // CORES) * count
            for l in range(lanes):
                returned_rows[l, row : row + count, :] = latent_in[p][
                    d, :, l * LANES : (l + 1) * LANES
                ].astype(jnp.float32)
        values = []
        for h in range(count):
            picked = jnp.concatenate(
                [returned_rows[l, pl.ds(h, n, stride=count), :] for l in range(lanes)], axis=1
            ).astype(jnp.bfloat16)
            values.append(
                jnp.dot(picked, value[first + h], preferred_element_type=jnp.float32).astype(
                    jnp.bfloat16
                )
            )
        values = jnp.concatenate(values, axis=1)
        for k in range(COLUMNS):
            product = jnp.dot(
                values,
                weight[first * vdim : end * vdim, k * span : (k + 1) * span],
                preferred_element_type=jnp.float32,
            )
            if first > 0:
                product = product + carried[:, k * span : (k + 1) * span]
            if end < heads:
                carried[:, k * span : (k + 1) * span] = product
            else:
                for c in range(CORES):
                    partial[s, k, c] = product[c * chips : (c + 1) * chips]
                pair(s, k).start()
                waiting.append((s, k))
            while len(waiting) > 1 or (waiting and end < heads):
                finish(*waiting.pop(0))
    while waiting:
        finish(*waiting.pop(0))

    for s in range(slots):
        partials_of[s][1]()
    for k in range(COLUMNS):
        sums = []
        for s in range(slots):
            summed = partial_in[s, k, 0].astype(jnp.float32)
            for e in range(1, chips):
                summed = summed + partial_in[s, k, e].astype(jnp.float32)
            sums.append(summed)
        for c in range(2):
            at = k * span + c * half
            out_ref[:, at : at + half] = jnp.concatenate(
                [summed[c : c + 1] for summed in sums], axis=0
            ).astype(jnp.bfloat16)
    for s in range(slots):
        for k in range(COLUMNS):
            pair(s, k).wait_send()
    for pending in queries_of + latents_of + partials_of:
        pending[2]()


def on_device(n, queries, absorb_key, absorb_value, out_weight, latent_cache, lengths, slot_request):
    cache = jnp.swapaxes(latent_cache, 1, 2)
    requests, heads, width = queries.shape
    slots, key_width, context = cache.shape
    nope, latent = absorb_key.shape[1:]
    model = out_weight.shape[1]
    rows = requests * heads
    chips = n // CORES
    pieces = pieces_of(slots, heads)
    span = model // COLUMNS
    vmem, anywhere = (pl.BlockSpec(memory_space=space) for space in (pltpu.VMEM, pltpu.HBM))
    low, wide = jnp.bfloat16, jnp.float32
    absorbed = [
        pltpu.VMEM((n, end - first, latent + (slots * (width - nope) if p == 0 else 0)), low)
        for p, (_, first, end) in enumerate(pieces)
    ]
    mixed = [pltpu.VMEM((n, end - first, latent), low) for _, first, end in pieces]
    per_piece = pltpu.SemaphoreType.DMA((len(pieces),))
    return pl.pallas_call(
        functools.partial(kernel, n, pieces),
        out_shape=jax.ShapeDtypeStruct((slots, model), low),
        in_specs=[anywhere] * 7,
        out_specs=vmem,
        scratch_shapes=[
            pltpu.SMEM(slot_request.shape, jnp.int32),
            pltpu.SMEM(lengths.shape, jnp.int32),
            pltpu.VMEM(queries.shape, low),
            pltpu.VMEM(absorb_key.shape, low),
            pltpu.VMEM(absorb_value.shape, low),
            pltpu.VMEM(out_weight.shape, low),
            pltpu.VMEM(cache.shape, low),
            pltpu.VMEM((rows, nope), wide),
            pltpu.VMEM((rows, width - nope), wide),
            pltpu.VMEM((latent // LANES, rows, LANES), wide),
            pltpu.VMEM((n * heads, key_width), wide),
            pltpu.VMEM((n * heads, context), wide),
            pltpu.VMEM((n * heads, latent), wide),
            pltpu.VMEM((latent // LANES, n * heads, LANES), wide),
            *absorbed,
            *absorbed,
            *mixed,
            *mixed,
            pltpu.VMEM((n, model), wide),
            pltpu.VMEM((slots, COLUMNS, CORES, chips, span), wide),
            pltpu.VMEM((slots, COLUMNS, chips, span), wide),
            pltpu.VMEM((slots, COLUMNS, chips, 2, span // 2), low),
            pltpu.VMEM((slots, COLUMNS, chips, 2, span // 2), low),
            pltpu.SemaphoreType.DMA((3,)),
            pltpu.SemaphoreType.DMA((3 + slots,)),
            per_piece,
            per_piece,
            per_piece,
            per_piece,
            pltpu.SemaphoreType.DMA((slots, COLUMNS)),
            pltpu.SemaphoreType.DMA((slots, COLUMNS)),
            pltpu.SemaphoreType.DMA((slots,)),
            pltpu.SemaphoreType.DMA((slots,)),
        ],
        compiler_params=pltpu.CompilerParams(
            collective_id=0, has_side_effects=True, vmem_limit_bytes=56000 * 1000
        ),
        name="decode",
    )(
        *(
            pltpu.with_memory_space_constraint(operand, pltpu.HBM)
            for operand in (slot_request, lengths, queries, absorb_key, absorb_value, out_weight, cache)
        )
    )


def solution(mesh):
    return jax.shard_map(
        functools.partial(on_device, mesh.shape["req"]),
        mesh=mesh,
        in_specs=(
            P("groups", "req", None),
            P("req", None, None),
            P("req", None, None),
            P("req", None),
            P(("groups", "req"), None, None),
            P(("groups", "req")),
            P("groups"),
        ),
        out_specs=P(("groups", "req"), None),
        check_vma=False,
    )
```

profile of v0, /device:TPU:0, one launch (start us, length us, event | category | flops | bytes accessed | tf_op | source)
XLA Modules:
  0.0 30.4 jit_solution(12583658651475200137)
XLA Ops:
  0.0 29.7 %decode.1 = bf16[2,5120]{1,0:T(2,128)(2,1)S(1)} custom-call(s32[32]{0:T(128)} %request_hbm.1, s32[2]{0:T(128)} %length_hbm.1, bf16[32,8,192]{2,1,0:T(8,128)(2,1)} %query_hbm.1, bf16[8,128,512]{2,1,0:T(8,128)(2,1)} %key_hbm.1, bf16[8,512,128]{2,1,0:T(8,128)(2,1)} %value_hbm.1, bf16[1024,5120]{1,0:T(8,128)(2,1)} %weight_hbm.1, bf16[2,576,4096]{2,1,0:T(8,128)(2,1)} %bitcast.1), custom_call_target="tpu_custom_call" | custom-call | tf_op jit(solution)/shard_map/decode/pallas_call | solution.py:310
  29.7 0.6 %copy.9 = bf16[2,5120]{1,0:T(2,128)(2,1)} copy(bf16[2,5120]{1,0:T(2,128)(2,1)S(1)} %decode.1) | data formatting | bytes 40960
where the time goes:
time: 30.5 us; the launch traced here: 30.4 us
  Pallas kernels  29.7 us (97%)
  local copies, waits for them, and re-layouts  0.61 us (2%)
    pallas_call x1, Pallas kernels, on_device(): pl.pallas_call(functools.partial(kernel, n, pieces), out_shape=jax.ShapeD...  29.7 us

commit v1 on v0

--- a/solution.py
+++ b/solution.py
@@ -13,6 +13,7 @@
 CORES = 2
 SCORE_TILE = 1024
 COLUMNS = 2
+STAGES = 4
 
 
 def pieces_of(slots, heads):
@@ -20,10 +21,12 @@
     return whole + [(slots - 1, 0, heads)]
 
 
-def far_first(mine, count, width):
+def far_first(mine, count, width, near_edges=False):
     block, place, blocks = lax.div(mine, width), lax.rem(mine, width), count // width
     low = (block < blocks // 2).astype(jnp.int32)
-    for i in range(blocks - 1):
+    edge = (block == 0).astype(jnp.int32) + (block == blocks - 1).astype(jnp.int32)
+    for step in range(blocks - 1):
+        i = lax.rem(step + edge * (blocks - 2), blocks - 1) if near_edges else step
         down = blocks - 1 - i - (blocks - 1 - i <= block).astype(jnp.int32)
         up = i + (i >= block).astype(jnp.int32)
         chosen = low * down + (1 - low) * up
@@ -96,7 +99,7 @@
                 :, l * LANES : (l + 1) * LANES
             ]
 
-    def exchange(out, into, send_sem, recv_sem, stride=1):
+    def exchange(out, into, send_sem, recv_sem, stride=1, near_edges=False):
         mine, count = lax.div(me, stride), n // stride
 
         def copy(to, source, block):
@@ -110,7 +113,7 @@
             )
 
         def start(*block):
-            for to in far_first(mine, count, 2 * CORES // stride):
+            for to in far_first(mine, count, 2 * CORES // stride, near_edges):
                 copy(to, mine, block).start()
 
         def others(ref):
@@ -126,10 +129,12 @@
         return start, arrive, leave
 
     queries_of = [
-        exchange(absorbed_out[p], absorbed_in[p], send_a.at[p], recv_a.at[p]) for p in range(parts)
+        exchange(absorbed_out[p], absorbed_in[p], send_a.at[p], recv_a.at[p], near_edges=p > 0)
+        for p in range(parts)
     ]
     latents_of = [
-        exchange(latent_out[p], latent_in[p], send_b.at[p], recv_b.at[p]) for p in range(parts)
+        exchange(latent_out[p], latent_in[p], send_b.at[p], recv_b.at[p])
+        for p in range(parts)
     ]
     partials_of = [
         exchange(partial_out.at[s], partial_in.at[s], send_c.at[s], recv_c.at[s], CORES)
@@ -171,7 +176,7 @@
         if first == 0:
             load_cache[s].wait()
         length = length_ref[s]
-        highest = None
+        tops = []
         for t in range(0, context, SCORE_TILE):
             score = jnp.dot(
                 query, cache[s, :, t : t + SCORE_TILE], preferred_element_type=jnp.float32
@@ -179,20 +184,29 @@
             position = t + lax.broadcasted_iota(jnp.int32, (1, SCORE_TILE), 1)
             score = jnp.where(position < length, score, -jnp.inf)
             scores[:rows, t : t + SCORE_TILE] = score
-            top = jnp.max(score, axis=1, keepdims=True)
-            highest = top if highest is None else jnp.maximum(highest, top)
-        total, mixed = None, None
-        for t in range(0, context, SCORE_TILE):
-            prob = jnp.exp2((scores[:rows, t : t + SCORE_TILE] - highest) * scale)
-            part = jnp.sum(prob, axis=1, keepdims=True)
-            product = lax.dot_general(
-                prob.astype(jnp.bfloat16),
-                cache[s, :latent, t : t + SCORE_TILE],
-                (((1,), (1,)), ((), ())),
-                preferred_element_type=jnp.float32,
-            )
-            total = part if total is None else total + part
-            mixed = product if mixed is None else mixed + product
+            tops.append(jnp.max(score, axis=1, keepdims=True))
+        highest, total, mixed = None, None, None
+        for stage in range(STAGES):
+            tiles = range(
+                stage * context // STAGES, (stage + 1) * context // STAGES, SCORE_TILE
+            )
+            top = functools.reduce(jnp.maximum, [tops[t // SCORE_TILE] for t in tiles])
+            if highest is not None:
+                top = jnp.maximum(highest, top)
+                keep = jnp.exp2((highest - top) * scale)
+                total, mixed = total * keep, mixed * keep
+            highest = top
+            for t in tiles:
+                prob = jnp.exp2((scores[:rows, t : t + SCORE_TILE] - highest) * scale)
+                part = jnp.sum(prob, axis=1, keepdims=True)
+                product = lax.dot_general(
+                    prob.astype(jnp.bfloat16),
+                    cache[s, :latent, t : t + SCORE_TILE],
+                    (((1,), (1,)), ((), ())),
+                    preferred_element_type=jnp.float32,
+                )
+                total = part if total is None else total + part
+                mixed = product if mixed is None else mixed + product
         latent_rows[:rows, :] = mixed / total
         for i in range(n):
             latent_out[p][i] = latent_rows[i * count : (i + 1) * count, :].astype(jnp.bfloat16)

time: 30.5 us -> 29.3 us (0.961)
  Pallas kernels: 29.7 us -> 28.6 us
    pallas_call x1, Pallas kernels: 29.7 us -> 28.6 us  [on_device(): pl.pallas_call(functools.partial(kernel, n, pieces), out_shape=jax.ShapeD...]
where the time goes in v1:
time: 29.3 us; the launch traced here: 29.2 us
  Pallas kernels  28.6 us (98%)
  local copies, waits for them, and re-layouts  0.61 us (2%)
    pallas_call x1, Pallas kernels, on_device(): pl.pallas_call(functools.partial(kernel, n, pieces), out_shape=jax.ShapeD...  28.6 us
    unnamed x1, local copies, waits for them, and re-layouts  0.61 us

profile of v1, /device:TPU:0, one launch (start us, length us, event | category | flops | bytes accessed | tf_op | source)
XLA Modules:
  0.0 29.2 jit_solution(17284335745022965554)
XLA Ops:
  0.0 28.6 %decode.1 = bf16[2,5120]{1,0:T(2,128)(2,1)S(1)} custom-call(s32[32]{0:T(128)} %request_hbm.1, s32[2]{0:T(128)} %length_hbm.1, bf16[32,8,192]{2,1,0:T(8,128)(2,1)} %query_hbm.1, bf16[8,128,512]{2,1,0:T(8,128)(2,1)} %key_hbm.1, bf16[8,512,128]{2,1,0:T(8,128)(2,1)} %value_hbm.1, bf16[1024,5120]{1,0:T(8,128)(2,1)} %weight_hbm.1, bf16[2,576,4096]{2,1,0:T(8,128)(2,1)} %bitcast.1), custom_call_target="tpu_custom_call" | custom-call | tf_op jit(solution)/shard_map/decode/pallas_call | solution.py:324
  28.6 0.6 %copy.9 = bf16[2,5120]{1,0:T(2,128)(2,1)} copy(bf16[2,5120]{1,0:T(2,128)(2,1)S(1)} %decode.1) | data formatting | bytes 40960

commit v2 on v1

--- a/solution.py
+++ b/solution.py
@@ -78,7 +78,6 @@
         for s in range(slots)
     ]
     load_key.start()
-    load_cache[0].start()
 
     for load in small:
         load.wait()
@@ -87,8 +86,8 @@
         query_rows[j * heads : (j + 1) * heads, :] = row[:, :nope]
         rotary_rows[j * heads : (j + 1) * heads, :] = row[:, nope:]
     load_key.wait()
-    for s in range(1, slots):
-        load_cache[s].start()
+    for load in load_cache:
+        load.start()
     load_value.start()
     load_weight.start()
     for h in range(heads):
@@ -207,9 +206,9 @@
                 )
                 total = part if total is None else total + part
                 mixed = product if mixed is None else mixed + product
-        latent_rows[:rows, :] = mixed / total
+        mixed = mixed * (1.0 / total)
         for i in range(n):
-            latent_out[p][i] = latent_rows[i * count : (i + 1) * count, :].astype(jnp.bfloat16)
+            latent_out[p][i] = mixed[i * count : (i + 1) * count, :].astype(jnp.bfloat16)
         latents_of[p][0]()
         latent_in[p][me] = latent_out[p][me]
 
@@ -282,19 +281,19 @@
     while waiting:
         finish(*waiting.pop(0))
 
+    sums = []
     for s in range(slots):
         partials_of[s][1]()
-    for k in range(COLUMNS):
-        sums = []
-        for s in range(slots):
+        for k in range(COLUMNS):
             summed = partial_in[s, k, 0].astype(jnp.float32)
             for e in range(1, chips):
                 summed = summed + partial_in[s, k, e].astype(jnp.float32)
             sums.append(summed)
+    for k in range(COLUMNS):
         for c in range(2):
             at = k * span + c * half
             out_ref[:, at : at + half] = jnp.concatenate(
-                [summed[c : c + 1] for summed in sums], axis=0
+                [summed[c : c + 1] for summed in sums[k::COLUMNS]], axis=0
             ).astype(jnp.bfloat16)
     for s in range(slots):
         for k in range(COLUMNS):

time: 29.3 us -> 29.3 us (level)
  no operation moved by 1% of the time
where the time goes in v2:
time: 29.3 us; the launch traced here: 29.2 us
  Pallas kernels  28.5 us (97%)
  local copies, waits for them, and re-layouts  0.61 us (2%)
    pallas_call x1, Pallas kernels, on_device(): pl.pallas_call(functools.partial(kernel, n, pieces), out_shape=jax.ShapeD...  28.5 us
    unnamed x1, local copies, waits for them, and re-layouts  0.61 us

profile of v2, /device:TPU:0, one launch (start us, length us, event | category | flops | bytes accessed | tf_op | source)
XLA Modules:
  0.0 29.2 jit_solution(2549578769883320354)
XLA Ops:
  0.0 28.5 %decode.1 = bf16[2,5120]{1,0:T(2,128)(2,1)S(1)} custom-call(s32[32]{0:T(128)} %request_hbm.1, s32[2]{0:T(128)} %length_hbm.1, bf16[32,8,192]{2,1,0:T(8,128)(2,1)} %query_hbm.1, bf16[8,128,512]{2,1,0:T(8,128)(2,1)} %key_hbm.1, bf16[8,512,128]{2,1,0:T(8,128)(2,1)} %value_hbm.1, bf16[1024,5120]{1,0:T(8,128)(2,1)} %weight_hbm.1, bf16[2,576,4096]{2,1,0:T(8,128)(2,1)} %bitcast.1), custom_call_target="tpu_custom_call" | custom-call | tf_op jit(solution)/shard_map/decode/pallas_call | solution.py:323
  28.5 0.6 %copy.9 = bf16[2,5120]{1,0:T(2,128)(2,1)} copy(bf16[2,5120]{1,0:T(2,128)(2,1)S(1)} %decode.1) | data formatting | bytes 40960
